TPU v7x, 256 devices: a whole 4x4x8 slice. The times are simulated.
256 devices in a mesh: seq: 64 (over z, y, core), head: 4 (over x).
Axes of the slice: x: 4, y: 4, z: 8, core: 2. Of those that a mesh axis runs over, the one named last changes fastest.
Arguments:
- rotated_query_rows: bfloat16 [32768, 4096], P(('seq', 'head')), may hold values from -8 to 8
- rotated_key_rows: bfloat16 [32768, 2048], P(('seq', 'head')), may hold values from -8 to 8
- value_matrix: bfloat16 [32768, 2048], P(('seq', 'head')), may hold values from -6 to 6
- output_gradient: bfloat16 [32768, 4096], P(('seq', 'head')), may hold values from -6 to 6
- doc_lengths: int32 [64], replicated, may hold values from 1 to 2048, 32768 in all
Outputs:
- attended: bfloat16 [32768, 4096], P(('seq', 'head'))
- query_grad: bfloat16 [32768, 4096], P(('seq', 'head'))
- key_gradient: bfloat16 [32768, 2048], P(('seq', 'head'))
- value_gradient: bfloat16 [32768, 2048], P(('seq', 'head'))
Inputs may be any that keep to these rules, and one draw needn't show every extreme that they name: `doc_lengths`: the lengths of the 64 documents packed in order; they sum to 32768 and the longest has 2048 tokens.
All inputs are finite; a program needn't handle non-finite values.
Results may differ from a plain program's by a relative error of at most 0.02.
Values may be sent and summed in bfloat16 or wider, within the bound.
A program may use at most 128 MiB of HBM per device.

v0:
```python
import jax
import jax.numpy as jnp
from jax import lax
from jax.sharding import PartitionSpec as P

HEAD_WIDTH = 256
WINDOW_LENGTH = 1024
query_tile = 512


def passed_along(block, axis, distance):
    devices = range(lax.axis_size(axis))
    route = [(i - distance, i) for i in devices if i - distance in devices]
    return lax.ppermute(block, axis, route)


def doc_index(positions, doc_lengths):
    starts = jnp.cumsum(doc_lengths) - doc_lengths
    counted = jnp.sum((starts[None, :] <= positions[:, None]).astype(jnp.int32), axis=1)
    return counted - 1


def tile_pass(
    query_block, grad_block, key_block, value_block, query_docs, query_place, key_docs, key_place
):
    score_scale = HEAD_WIDTH ** (-0.5)
    scores = (
        jnp.einsum("qgd,kd->gqk", query_block, key_block, preferred_element_type=jnp.float32)
        * score_scale
    )
    offsets = query_place[:, None] - key_place[None, :]
    visible = (
        (query_docs[:, None] == key_docs[None, :]) & (offsets >= 0) & (offsets < WINDOW_LENGTH)
    )
    scores = jnp.where(visible[None], scores, -jnp.inf)
    row_max = jnp.max(scores, axis=2, keepdims=True)
    weights = jnp.exp(scores - row_max)
    probs_full = weights / jnp.sum(weights, axis=2, keepdims=True)
    probs_low = probs_full.astype(jnp.bfloat16)
    attended = jnp.einsum(
        "gqk,kd->qgd", probs_low, value_block, preferred_element_type=jnp.float32
    ).astype(jnp.bfloat16)
    row_delta = jnp.sum(grad_block.astype(jnp.float32) * attended.astype(jnp.float32), axis=2)
    value_part = jnp.einsum(
        "gqk,qgd->kd", probs_low, grad_block, preferred_element_type=jnp.float32
    )
    grad_probs = jnp.einsum(
        "qgd,kd->gqk", grad_block, value_block, preferred_element_type=jnp.float32
    )
    grad_low = (probs_full * (grad_probs - jnp.transpose(row_delta)[:, :, None])).astype(
        jnp.bfloat16
    )
    query_grad = (
        jnp.einsum("gqk,kd->qgd", grad_low, key_block, preferred_element_type=jnp.float32)
        * score_scale
    ).astype(jnp.bfloat16)
    key_part = (
        jnp.einsum("gqk,qgd->kd", grad_low, query_block, preferred_element_type=jnp.float32)
        * score_scale
    )
    return (attended, query_grad, key_part, value_part)


def head_sweep(query_head, grad_head, kv_head, key_docs, key_place, own_start):
    block_rows = query_head.shape[0]
    tile_rows = min(block_rows, query_tile)
    finish = own_start + tile_rows
    key_start = finish - tile_rows - WINDOW_LENGTH
    results = tile_pass(
        query_head,
        grad_head,
        kv_head[0, key_start:finish],
        kv_head[1, key_start:finish],
        key_docs[own_start:finish],
        key_place[own_start:finish],
        key_docs,
        key_place,
    )
    attended_tiles = results[0]
    grad_tiles = results[1]
    key_gradient_sums = results[2]
    value_gradient_sums = results[3]
    return (attended_tiles, grad_tiles, key_gradient_sums, value_gradient_sums)


def attend(exchanged, doc_lengths, group_width):
    query_parts, key_parts, value_parts, grad_parts = exchanged
    block_rows = query_parts.shape[0]
    head_items = query_parts.shape[2]
    kv_block = jnp.stack([key_parts[:, 0], value_parts[:, 0]], axis=0)
    rim_count = (WINDOW_LENGTH + block_rows - 2) // block_rows
    margin = max(0, WINDOW_LENGTH - rim_count * block_rows)
    rim_blocks = [passed_along(kv_block, "seq", distance) for distance in range(1, rim_count + 1)]
    pieces = (
        [jnp.zeros((2, margin, head_items, HEAD_WIDTH), jnp.bfloat16)]
        + rim_blocks[::-1]
        + [kv_block]
    )
    kv_window = jnp.concatenate(pieces, axis=1)
    own_start = margin + rim_count * block_rows
    key_length = own_start + block_rows
    key_place = (
        lax.axis_index("seq") * block_rows - own_start + jnp.arange(key_length, dtype=jnp.int32)
    )
    key_docs = doc_index(key_place, doc_lengths)
    outputs = []
    for head_item in range(head_items):
        query_head = query_parts[:, 0, head_item].reshape(block_rows, group_width, HEAD_WIDTH)
        grad_head = grad_parts[:, 0, head_item].reshape(block_rows, group_width, HEAD_WIDTH)
        kv_head = kv_window[:, :, head_item]
        swept_head = head_sweep(query_head, grad_head, kv_head, key_docs, key_place, own_start)
        outputs.append(swept_head)
    attended = jnp.stack([swept_head[0] for swept_head in outputs], axis=1).reshape(
        block_rows, 1, head_items, group_width * HEAD_WIDTH
    )
    query_grad = jnp.stack([swept_head[1] for swept_head in outputs], axis=1).reshape(
        block_rows, 1, head_items, group_width * HEAD_WIDTH
    )
    partial_grads = jnp.stack(
        [jnp.stack([swept_head[2], swept_head[3]], axis=0) for swept_head in outputs], axis=2
    )
    own_part = partial_grads[:, own_start:]
    gathered = own_part
    for distance in range(1, rim_count + 1):
        gathered = gathered + passed_along(
            partial_grads[
                :, own_start - distance * block_rows : own_start - (distance - 1) * block_rows
            ],
            "seq",
            -distance,
        )
    key_gradient = gathered[0].astype(jnp.bfloat16)[:, None]
    value_gradient = gathered[1].astype(jnp.bfloat16)[:, None]
    return (
        lax.all_to_all(attended, "head", split_axis=0, concat_axis=1, tiled=True),
        lax.all_to_all(query_grad, "head", split_axis=0, concat_axis=1, tiled=True),
        lax.all_to_all(key_gradient, "head", split_axis=0, concat_axis=1, tiled=True),
        lax.all_to_all(value_gradient, "head", split_axis=0, concat_axis=1, tiled=True),
    )


def shards(rotated_query_rows, rotated_key_rows, value_matrix, output_gradient, doc_lengths):
    token_total = rotated_query_rows.shape[0]
    groups_count = lax.axis_size("head")
    kv_count = rotated_key_rows.shape[1] // HEAD_WIDTH
    per_device = kv_count // groups_count
    group_width = rotated_query_rows.shape[1] // rotated_key_rows.shape[1]
    query_split = rotated_query_rows.reshape(
        token_total, groups_count, per_device, group_width * HEAD_WIDTH
    )
    key_split = rotated_key_rows.reshape(token_total, groups_count, per_device, HEAD_WIDTH)
    value_split = value_matrix.reshape(token_total, groups_count, per_device, HEAD_WIDTH)
    grad_split = output_gradient.reshape(
        token_total, groups_count, per_device, group_width * HEAD_WIDTH
    )
    attended, query_grad, key_gradient, value_gradient = attend(
        (
            lax.all_to_all(query_split, "head", split_axis=1, concat_axis=0, tiled=True),
            lax.all_to_all(key_split, "head", split_axis=1, concat_axis=0, tiled=True),
            lax.all_to_all(value_split, "head", split_axis=1, concat_axis=0, tiled=True),
            lax.all_to_all(grad_split, "head", split_axis=1, concat_axis=0, tiled=True),
        ),
        doc_lengths,
        group_width,
    )
    return (
        attended.reshape(token_total, rotated_query_rows.shape[1]),
        query_grad.reshape(token_total, rotated_query_rows.shape[1]),
        key_gradient.reshape(token_total, rotated_key_rows.shape[1]),
        value_gradient.reshape(token_total, rotated_key_rows.shape[1]),
    )


def solution(mesh):
    in_specs = (
        P(("seq", "head"), None),
        P(("seq", "head"), None),
        P(("seq", "head"), None),
        P(("seq", "head"), None),
        P(),
    )
    out_specs = (
        P(("seq", "head"), None),
        P(("seq", "head"), None),
        P(("seq", "head"), None),
        P(("seq", "head"), None),
    )
    return jax.shard_map(shards, mesh=mesh, in_specs=in_specs, out_specs=out_specs, check_vma=False)
```

profile of v0, /device:TPU:122, one launch (start us, length us, event | category | flops | bytes accessed | tf_op | source)
XLA Modules:
  0.0 237.3 jit_solution(12690508888914768315)
XLA Ops:
  0.7 1.4 copy.159
  2.1 1.0 copy.160
  3.1 4.8 %all-to-all-start = ((bf16[128,4,2,256]{3,0,2,1:T(8,128)(2,1)}), bf16[128,4,2,256]{3,0,2,1:T(8,128)(2,1)S(1)}, u32[]{:S(2)}, u32[]{:S(2)}) async-start(bf16[128,4,2,256]{3,0,2,1:T(8,128)(2,1)} %copy.160), calls=%async_computation | async-start | bytes 1048576 | tf_op jit(solution)/shard_map/all_to_all | solution.py:159
  9.2 6.7 %all-to-all-done = bf16[128,4,2,256]{3,0,2,1:T(8,128)(2,1)S(1)} async-done(((bf16[128,4,2,256]{3,0,2,1:T(8,128)(2,1)}), bf16[128,4,2,256]{3,0,2,1:T(8,128)(2,1)S(1)}, u32[]{:S(2)}, u32[]{:S(2)}) %all-to-all-start) | async-done | bytes 524320 | tf_op jit(solution)/shard_map/all_to_all | solution.py:159
  15.9 4.9 %all-to-all-start.1 = ((bf16[128,4,2,256]{3,0,2,1:T(8,128)(2,1)}), bf16[128,4,2,256]{3,0,2,1:T(8,128)(2,1)S(1)}, u32[]{:S(2)}, u32[]{:S(2)}) async-start(bf16[128,4,2,256]{3,0,2,1:T(8,128)(2,1)} %copy.163), calls=%async_computation.1 | async-start | bytes 1048576 | tf_op jit(solution)/shard_map/all_to_all | solution.py:160
  20.8 1.3 copy.166
  22.1 5.5 %all-to-all-done.1 = bf16[128,4,2,256]{3,0,2,1:T(8,128)(2,1)S(1)} async-done(((bf16[128,4,2,256]{3,0,2,1:T(8,128)(2,1)}), bf16[128,4,2,256]{3,0,2,1:T(8,128)(2,1)S(1)}, u32[]{:S(2)}, u32[]{:S(2)}) %all-to-all-start.1) | async-done | bytes 524320 | tf_op jit(solution)/shard_map/all_to_all | solution.py:160
  27.7 4.9 %all-to-all-start.2 = ((bf16[128,4,2,512]{0,3,2,1:T(8,128)(2,1)}), bf16[128,4,2,512]{0,3,2,1:T(8,128)(2,1)S(1)}, u32[]{:S(2)}, u32[]{:S(2)}) async-start(bf16[128,4,2,512]{0,3,2,1:T(8,128)(2,1)} %bitcast.13), calls=%async_computation.2 | async-start | bytes 2097152 | tf_op jit(solution)/shard_map/all_to_all | solution.py:158
  33.1 1.6 copy.179
  34.7 2.0 copy.180
  36.8 1.3 copy.164
  38.1 5.7 %all-to-all-done.2 = bf16[128,4,2,512]{0,3,2,1:T(8,128)(2,1)S(1)} async-done(((bf16[128,4,2,512]{0,3,2,1:T(8,128)(2,1)}), bf16[128,4,2,512]{0,3,2,1:T(8,128)(2,1)S(1)}, u32[]{:S(2)}, u32[]{:S(2)}) %all-to-all-start.2) | async-done | bytes 1048608 | tf_op jit(solution)/shard_map/all_to_all | solution.py:158
  43.8 5.1 %all-to-all-start.4 = ((bf16[128,4,2,512]{3,2,0,1:T(2,128)(2,1)}), bf16[128,4,2,512]{3,2,0,1:T(2,128)(2,1)S(1)}, u32[]{:S(2)}, u32[]{:S(2)}) async-start(bf16[128,4,2,512]{3,2,0,1:T(2,128)(2,1)} %copy.180), calls=%async_computation.4 | async-start | bytes 2097152 | tf_op jit(solution)/shard_map/all_to_all | solution.py:161
  48.9 1.1 pad_maximum_fusion.1
  50.0 1.9 collective-permute-start.1
  51.9 4.7 %collective-permute-start = (bf16[2,512,2,256]{3,1,2,0:T(8,128)(2,1)}, bf16[2,512,2,256]{3,1,2,0:T(8,128)(2,1)}, u32[]{:S(2)}, u32[]{:S(2)}) collective-permute-start(bf16[2,512,2,256]{3,1,2,0:T(8,128)(2,1)} %pad_maximum_fusion.1), channel_id=1, source_target_pairs={{0,8},{4,12},{8,16},{12,20},{16,24},{20,28},{24,32},{28,36},{32,40... | collective-permute-start | bytes 3145736 | tf_op jit(solution)/shard_map/ppermute | solution.py:14
  56.7 2.1 fusion.13
  58.8 1.3 copy.167
  60.1 1.3 fusion.40
  63.4 1.5 fusion.39
  64.9 2.3 copy.220
  67.1 2.3 copy.221
  69.4 5.7 %collective-permute-done.1 = bf16[2,512,2,256]{3,1,2,0:T(8,128)(2,1)} collective-permute-done((bf16[2,512,2,256]{3,1,2,0:T(8,128)(2,1)}, bf16[2,512,2,256]{3,1,2,0:T(8,128)(2,1)}, u32[]{:S(2)}, u32[]{:S(2)}) %collective-permute-start.1) | collective-permute-done | bytes 1048608 | tf_op jit(solution)/shard_map/ppermute | solution.py:14
  75.1 5.4 %collective-permute-done = bf16[2,512,2,256]{3,1,2,0:T(8,128)(2,1)} collective-permute-done((bf16[2,512,2,256]{3,1,2,0:T(8,128)(2,1)}, bf16[2,512,2,256]{3,1,2,0:T(8,128)(2,1)}, u32[]{:S(2)}, u32[]{:S(2)}) %collective-permute-start) | collective-permute-done | bytes 1048608 | tf_op jit(solution)/shard_map/ppermute | solution.py:14
  80.5 2.1 maximum_maximum_fusion
  82.7 7.3 %fusion.42 = (f32[2,512]{1,0:T(2,128)S(1)}, f32[2,512,1536]{1,2,0:T(8,128)}) fusion(pred[512,1536]{0,1:T(8,128)(4,1)} %fusion.13, bf16[512,2,256]{0,2,1:T(8,128)(2,1)} %bitcast.208, bf16[2,1536,2,256]{3,1,2,0:T(8,128)(2,1)S(1)} %maximum_maximum_fusion), kind=kOutput, calls=%fused_computation.80 | convolution fusion | flops 811599360 | bytes 8392704 | tf_op jit(solution)/shard_map/sub | solution.py:37
  90.0 3.7 %fusion.20 = bf16[2,512,1536]{1,2,0:T(8,128)(2,1)S(1)} fusion(f32[2,512,1536]{1,2,0:T(8,128)} %get-tuple-element.15, f32[2,512]{1,0:T(2,128)S(1)} %get-tuple-element.14), kind=kLoop, calls=%fused_computation.41 | loop fusion | flops 3145728 | bytes 9441280 | tf_op jit(solution)/shard_map/convert_element_type | solution.py:39
  93.7 1.8 multiply_reduce_fusion.1
  95.6 2.2 convolution_bitcast_fusion.2
  97.7 6.3 %fusion.41 = (f32[2,512]{1,0:T(2,128)S(1)}, f32[2,512,1536]{1,2,0:T(8,128)}) fusion(pred[512,1536]{0,1:T(8,128)(4,1)} %fusion.13, bf16[512,2,256]{0,2,1:T(8,128)(2,1)} %bitcast.206, bf16[2,1536,2,256]{3,1,2,0:T(8,128)(2,1)S(1)} %maximum_maximum_fusion), kind=kOutput, calls=%fused_computation.79 | convolution fusion | flops 811599360 | bytes 8392704 | tf_op jit(solution)/shard_map/sub | solution.py:37
  104.0 3.8 %fusion.21 = bf16[2,512,1536]{1,2,0:T(8,128)(2,1)S(1)} fusion(f32[2,512,1536]{1,2,0:T(8,128)} %get-tuple-element.13, f32[2,512]{1,0:T(2,128)S(1)} %get-tuple-element.12), kind=kLoop, calls=%fused_computation.42 | loop fusion | flops 3145728 | bytes 9441280 | tf_op jit(solution)/shard_map/convert_element_type | solution.py:39
  107.9 1.8 multiply_reduce_fusion
  110.8 1.1 fusion.5
  112.2 1.0 fusion.19
  113.8 1.2 fusion.3
  115.1 1.7 copy-done.5
  116.8 1.0 fusion.17
  118.6 2.7 %fusion.22 = (f32[2,512,2,256]{3,1,0,2:T(8,128)}, f32[2,512,2,256]{3,1,0,2:T(8,128)}) fusion(f32[2,1536,1,256]{3,1,0,2:T(8,128)S(1)} %get-tuple-element.20, f32[2,1536,1,256]{3,1,0,2:T(8,128)S(1)} %get-tuple-element.21), kind=kLoop, calls=%fused_computation.43 | loop fusion | flops 1048576 | bytes 10485760 | tf_op jit(solution)/shard_map/stack | solution.py:119
  121.6 10.4 %collective-permute-start.2 = (f32[2,512,2,256]{3,1,0,2:T(8,128)}, f32[2,512,2,256]{3,1,0,2:T(8,128)}, u32[]{:S(2)}, u32[]{:S(2)}) collective-permute-start(f32[2,512,2,256]{3,1,0,2:T(8,128)} %get-tuple-element.4), channel_id=1, source_target_pairs={{4,0},{8,4},{12,8},{16,12},{20,16},{24,20},{28,24},{32,28},{36,32}... | collective-permute-start | bytes 6291464 | tf_op jit(solution)/shard_map/ppermute | solution.py:14
  132.0 2.4 collective-permute-start.3
  134.4 3.6 %copy.176 = bf16[512,1,1,512]{3,2,1,0:T(2,128)(2,1)} copy(bf16[512,1,1,512]{0,3,2,1:T(8,128)(2,1)} %bitcast.198) | data formatting | bytes 1048576 | tf_op jit(solution)/shard_map/stack | solution.py:113
  137.9 3.6 %copy.177 = bf16[512,1,1,512]{3,2,1,0:T(2,128)(2,1)} copy(bf16[512,1,1,512]{0,3,2,1:T(8,128)(2,1)} %bitcast.202) | data formatting | bytes 1048576 | tf_op jit(solution)/shard_map/stack | solution.py:113
  141.5 4.2 %pad_maximum_fusion.2 = bf16[512,1,2,512]{3,2,1,0:T(2,128)(2,1)} fusion(bf16[512,1,1,512]{3,2,1,0:T(2,128)(2,1)} %copy.177, bf16[512,1,1,512]{3,2,1,0:T(2,128)(2,1)} %copy.176), kind=kLoop, calls=%fused_computation.56 | loop fusion | flops 2097152 | bytes 2097152 | tf_op jit(solution)/shard_map/stack | solution.py:113
  145.7 4.8 %all-to-all-start.3 = ((bf16[512,1,2,512]{3,2,1,0:T(2,128)(2,1)}), bf16[512,1,2,512]{3,2,1,0:T(2,128)(2,1)}, u32[]{:S(2)}, u32[]{:S(2)}) async-start(bf16[512,1,2,512]{3,2,1,0:T(2,128)(2,1)} %pad_maximum_fusion.2), calls=%async_computation.3 | async-start | bytes 2097152 | tf_op jit(solution)/shard_map/all_to_all | solution.py:135
  150.5 3.9 %fusion.27 = bf16[256,2,512]{2,0,1:T(8,128)(2,1)} fusion(bf16[2,512,1536]{1,2,0:T(8,128)(2,1)} %copy-done.4, bf16[2,1536,2,256]{3,1,2,0:T(8,128)(2,1)} %copy-done.1), kind=kOutput, calls=%fused_computation.51 | convolution fusion | flops 805830656 | bytes 4456448 | tf_op jit(solution)/shard_map/gqk,kd->qgd/dot_general | solution.py:54
  154.4 3.6 %copy.189 = bf16[512,1,1,512]{3,2,1,0:T(2,128)(2,1)} copy(bf16[512,1,1,512]{0,3,2,1:T(8,128)(2,1)} %bitcast.191) | data formatting | bytes 1048576 | tf_op jit(solution)/shard_map/stack | solution.py:116
  158.0 3.9 %fusion.28 = bf16[256,2,512]{2,0,1:T(8,128)(2,1)} fusion(bf16[2,512,1536]{1,2,0:T(8,128)(2,1)} %copy-done.5, bf16[2,1536,2,256]{3,1,2,0:T(8,128)(2,1)} %copy-done.1), kind=kOutput, calls=%fused_computation.52 | convolution fusion | flops 805830656 | bytes 4456448 | tf_op jit(solution)/shard_map/gqk,kd->qgd/dot_general | solution.py:54
  161.9 3.6 %copy.190 = bf16[512,1,1,512]{3,2,1,0:T(2,128)(2,1)} copy(bf16[512,1,1,512]{0,3,2,1:T(8,128)(2,1)} %bitcast.190) | data formatting | bytes 1048576 | tf_op jit(solution)/shard_map/stack | solution.py:116
  165.5 4.2 %pad_maximum_fusion.3 = bf16[512,1,2,512]{3,2,1,0:T(2,128)(2,1)} fusion(bf16[512,1,1,512]{3,2,1,0:T(2,128)(2,1)} %copy.190, bf16[512,1,1,512]{3,2,1,0:T(2,128)(2,1)} %copy.189), kind=kLoop, calls=%fused_computation.57 | loop fusion | flops 2097152 | bytes 2097152 | tf_op jit(solution)/shard_map/stack | solution.py:116
  169.7 4.8 %all-to-all-start.5 = ((bf16[512,1,2,512]{3,2,1,0:T(2,128)(2,1)}), bf16[512,1,2,512]{3,2,1,0:T(2,128)(2,1)}, u32[]{:S(2)}, u32[]{:S(2)}) async-start(bf16[512,1,2,512]{3,2,1,0:T(2,128)(2,1)} %pad_maximum_fusion.3), calls=%async_computation.5 | async-start | bytes 2097152 | tf_op jit(solution)/shard_map/all_to_all | solution.py:136
  174.5 2.3 collective-permute-done.2
  176.7 29.7 %collective-permute-done.3 = f32[2,512,2,256]{3,1,0,2:T(8,128)} collective-permute-done((f32[2,512,2,256]{3,1,0,2:T(8,128)}, f32[2,512,2,256]{3,1,0,2:T(8,128)}, u32[]{:S(2)}, u32[]{:S(2)}) %collective-permute-start.3) | collective-permute-done | bytes 2097184 | tf_op jit(solution)/shard_map/ppermute | solution.py:14
  206.4 2.8 %fusion.26 = bf16[2,512,2,256]{3,1,0,2:T(8,128)(2,1)S(1)} fusion(f32[2,512,2,256]{3,1,0,2:T(8,128)} %collective-permute-done.3, f32[2,512,2,256]{3,1,0,2:T(8,128)} %collective-permute-done.2, f32[2,1536,1,256]{3,1,0,2:T(8,128)S(1)} %get-tuple-element.20, f32[2,1536,1,256]{3,1,0,2:T(8,128)} %copy-done), kind=kLoop, calls=%fused_computation.47 | loop fusion | flops 2097152 | bytes 11534336 | tf_op jit(solution)/shard_map/convert.1
  209.4 1.3 copy.198
  210.7 4.8 %all-to-all-start.7 = ((bf16[512,1,2,256]{3,2,1,0:T(2,128)(2,1)}), bf16[512,1,2,256]{3,2,1,0:T(2,128)(2,1)S(1)}, u32[]{:S(2)}, u32[]{:S(2)}) async-start(bf16[512,1,2,256]{3,2,1,0:T(2,128)(2,1)} %copy.198), calls=%async_computation.7 | async-start | bytes 1048576 | tf_op jit(solution)/shard_map/all_to_all | solution.py:138
  215.5 1.3 copy.196
  216.8 5.3 %all-to-all-done.7 = bf16[512,1,2,256]{3,2,1,0:T(2,128)(2,1)S(1)} async-done(((bf16[512,1,2,256]{3,2,1,0:T(2,128)(2,1)}), bf16[512,1,2,256]{3,2,1,0:T(2,128)(2,1)S(1)}, u32[]{:S(2)}, u32[]{:S(2)}) %all-to-all-start.7) | async-done | bytes 524320 | tf_op jit(solution)/shard_map/all_to_all | solution.py:138
  222.1 4.9 %all-to-all-start.6 = ((bf16[512,1,2,256]{3,2,1,0:T(2,128)(2,1)}), bf16[512,1,2,256]{3,2,1,0:T(2,128)(2,1)S(1)}, u32[]{:S(2)}, u32[]{:S(2)}) async-start(bf16[512,1,2,256]{3,2,1,0:T(2,128)(2,1)} %copy.196), calls=%async_computation.6 | async-start | bytes 1048576 | tf_op jit(solution)/shard_map/all_to_all | solution.py:137
  227.0 1.9 copy.178
  229.0 1.6 reshape.183
  230.6 1.9 copy.191
  232.5 1.6 reshape.185
  234.5 1.2 reshape.187
  236.1 1.2 reshape.186
  (74 shorter events, 7.6 us)
Async XLA Ops:
  0.6 7.3 %copy-start.12 = (bf16[128,2048]{1,0:T(8,128)(2,1)S(1)}, bf16[128,2048]{1,0:T(8,128)(2,1)}, u32[]{:S(2)}) copy-start(bf16[128,2048]{1,0:T(8,128)(2,1)} %param.7) | copy-start | bytes 1572868
  0.6 20.2 %copy-start.11 = (bf16[128,4096]{1,0:T(8,128)(2,1)S(1)}, bf16[128,4096]{1,0:T(8,128)(2,1)}, u32[]{:S(2)}) copy-start(bf16[128,4096]{1,0:T(8,128)(2,1)} %param.5) | copy-start | bytes 3145732
  3.1 12.8 %all-to-all-start = ((bf16[128,4,2,256]{3,0,2,1:T(8,128)(2,1)}), bf16[128,4,2,256]{3,0,2,1:T(8,128)(2,1)S(1)}, u32[]{:S(2)}, u32[]{:S(2)}) async-start(bf16[128,4,2,256]{3,0,2,1:T(8,128)(2,1)} %copy.160), calls=%async_computation | async-start | bytes 1048576 | tf_op jit(solution)/shard_map/all_to_all | solution.py:159
  8.2 24.4 %copy-start.19 = (s32[64]{0:T(128)S(1)}, s32[64]{0:T(128)}, u32[]{:S(2)}) copy-start(s32[64]{0:T(128)} %param.9) | copy-start | bytes 772
  15.9 11.7 %all-to-all-start.1 = ((bf16[128,4,2,256]{3,0,2,1:T(8,128)(2,1)}), bf16[128,4,2,256]{3,0,2,1:T(8,128)(2,1)S(1)}, u32[]{:S(2)}, u32[]{:S(2)}) async-start(bf16[128,4,2,256]{3,0,2,1:T(8,128)(2,1)} %copy.163), calls=%async_computation.1 | async-start | bytes 1048576 | tf_op jit(solution)/shard_map/all_to_all | solution.py:160
  27.7 5.4 %copy-start.6 = (bf16[128,4,2,256]{3,0,2,1:T(8,128)(2,1)}, bf16[128,4,2,256]{3,0,2,1:T(8,128)(2,1)S(1)}, u32[]{:S(2)}) copy-start(bf16[128,4,2,256]{3,0,2,1:T(8,128)(2,1)S(1)} %all-to-all-done.1) | copy-start | bytes 1572868
  27.7 16.2 %all-to-all-start.2 = ((bf16[128,4,2,512]{0,3,2,1:T(8,128)(2,1)}), bf16[128,4,2,512]{0,3,2,1:T(8,128)(2,1)S(1)}, u32[]{:S(2)}, u32[]{:S(2)}) async-start(bf16[128,4,2,512]{0,3,2,1:T(8,128)(2,1)} %bitcast.13), calls=%async_computation.2 | async-start | bytes 2097152 | tf_op jit(solution)/shard_map/all_to_all | solution.py:158
  32.6 5.4 %copy-start.15 = (s32[1536]{0:T(1024)}, s32[1536]{0:T(1024)S(1)}, u32[]{:S(2)}) copy-start(s32[1536]{0:T(1024)S(1)} %iota_add_fusion) | copy-start | bytes 18436
  33.1 5.0 %copy-start.17 = (s32[1536]{0:T(1024)}, s32[1536]{0:T(1024)S(1)}, u32[]{:S(2)}) copy-start(s32[1536]{0:T(1024)S(1)} %broadcast_add_fusion) | copy-start | bytes 18436
  36.8 23.3 %copy-start.2 = (bf16[4,128,1,2,256]{4,1,0,3,2:T(8,128)(2,1)}, bf16[4,128,1,2,256]{4,1,0,3,2:T(8,128)(2,1)S(1)}, u32[]{:S(2)}) copy-start(bf16[4,128,1,2,256]{4,1,0,3,2:T(8,128)(2,1)S(1)} %copy.161) | copy-start | bytes 1572868
  38.1 22.0 %copy-start.3 = (bf16[4,128,1,2,256]{4,1,0,3,2:T(8,128)(2,1)}, bf16[4,128,1,2,256]{4,1,0,3,2:T(8,128)(2,1)S(1)}, u32[]{:S(2)}) copy-start(bf16[4,128,1,2,256]{4,1,0,3,2:T(8,128)(2,1)S(1)} %copy.164) | copy-start | bytes 1572868
  43.8 12.8 %copy-start.16 = (s32[1536]{0:T(1024)S(1)}, s32[1536]{0:T(1024)}, u32[]{:S(2)}) copy-start(s32[1536]{0:T(1024)} %copy-done.15) | copy-start | bytes 18436
  43.8 12.8 %slice-start.4 = ((s32[1536]{0:T(1024)}), s32[512]{0:T(512)S(1)}, s32[]{:S(2)}) async-start(s32[1536]{0:T(1024)} %copy-done.15), calls=%async_computation.12 | async-start | bytes 4096 | tf_op jit(solution)/shard_map/slice | solution.py:75
  43.8 12.8 %copy-start.18 = (s32[1536]{0:T(1024)S(1)}, s32[1536]{0:T(1024)}, u32[]{:S(2)}) copy-start(s32[1536]{0:T(1024)} %copy-done.17) | copy-start | bytes 18436
  43.8 12.8 %slice-start.5 = ((s32[1536]{0:T(1024)}), s32[512]{0:T(512)S(1)}, s32[]{:S(2)}) async-start(s32[1536]{0:T(1024)} %copy-done.17), calls=%async_computation.13 | async-start | bytes 4096 | tf_op jit(solution)/shard_map/slice | solution.py:74
  43.8 19.5 %all-to-all-start.4 = ((bf16[128,4,2,512]{3,2,0,1:T(2,128)(2,1)}), bf16[128,4,2,512]{3,2,0,1:T(2,128)(2,1)S(1)}, u32[]{:S(2)}, u32[]{:S(2)}) async-start(bf16[128,4,2,512]{3,2,0,1:T(2,128)(2,1)} %copy.180), calls=%async_computation.4 | async-start | bytes 2097152 | tf_op jit(solution)/shard_map/all_to_all | solution.py:161
  50.0 25.1 %collective-permute-start.1 = (bf16[2,512,2,256]{3,1,2,0:T(8,128)(2,1)}, bf16[2,512,2,256]{3,1,2,0:T(8,128)(2,1)}, u32[]{:S(2)}, u32[]{:S(2)}) collective-permute-start(bf16[2,512,2,256]{3,1,2,0:T(8,128)(2,1)} %pad_maximum_fusion.1), channel_id=1, source_target_pairs={{0,4},{4,8},{8,12},{12,16},{16,20},{20,24},{24,28},{28,32},{32,36}... | collective-permute-start | bytes 3145736 | tf_op jit(solution)/shard_map/ppermute | solution.py:14
  51.9 28.6 %collective-permute-start = (bf16[2,512,2,256]{3,1,2,0:T(8,128)(2,1)}, bf16[2,512,2,256]{3,1,2,0:T(8,128)(2,1)}, u32[]{:S(2)}, u32[]{:S(2)}) collective-permute-start(bf16[2,512,2,256]{3,1,2,0:T(8,128)(2,1)} %pad_maximum_fusion.1), channel_id=1, source_target_pairs={{0,8},{4,12},{8,16},{12,20},{16,24},{20,28},{24,32},{28,36},{32,40... | collective-permute-start | bytes 3145736 | tf_op jit(solution)/shard_map/ppermute | solution.py:14
  82.7 31.1 %copy-start.1 = (bf16[2,1536,2,256]{3,1,2,0:T(8,128)(2,1)}, bf16[2,1536,2,256]{3,1,2,0:T(8,128)(2,1)S(1)}, u32[]{:S(2)}) copy-start(bf16[2,1536,2,256]{3,1,2,0:T(8,128)(2,1)S(1)} %maximum_maximum_fusion) | copy-start | bytes 9437188
  90.0 3.7 %copy-start.8 = (bf16[512,1,1,512]{0,3,2,1:T(8,128)(2,1)S(1)}, bf16[512,1,1,512]{0,3,2,1:T(8,128)(2,1)}, u32[]{:S(2)}) copy-start(bf16[512,1,1,512]{0,3,2,1:T(8,128)(2,1)} %copy.220) | copy-start | bytes 1572868
  104.0 3.9 %copy-start.7 = (bf16[512,1,1,512]{0,3,2,1:T(8,128)(2,1)S(1)}, bf16[512,1,1,512]{0,3,2,1:T(8,128)(2,1)}, u32[]{:S(2)}) copy-start(bf16[512,1,1,512]{0,3,2,1:T(8,128)(2,1)} %copy.221) | copy-start | bytes 1572868
  104.0 6.7 %slice-start = ((s8[6291456]{0:T(1024)(128)(4,1)}), s8[4194304]{0:T(1024)(128)(4,1)S(1)}, s32[]{:S(2)}) async-start(s8[6291456]{0:T(1024)(128)(4,1)} %bitcast.179), calls=%async_computation.8 | async-start | bytes 8388608
  107.9 2.8 %slice-start.1 = ((s8[6291456]{0:T(1024)(128)(4,1)}), s8[2097152]{0:T(1024)(128)(4,1)S(1)}, s32[]{:S(2)}) async-start(s8[6291456]{0:T(1024)(128)(4,1)} %bitcast.179), calls=%async_computation.9 | async-start | bytes 4194304
  109.7 1.0 copy-start.9
  109.7 4.1 %slice-start.2 = ((s8[6291456]{0:T(1024)(128)(4,1)}), s8[4194304]{0:T(1024)(128)(4,1)S(1)}, s32[]{:S(2)}) async-start(s8[6291456]{0:T(1024)(128)(4,1)} %bitcast.181), calls=%async_computation.10 | async-start | bytes 8388608
  110.8 1.4 copy-start.14
  110.8 3.1 %slice-start.3 = ((s8[6291456]{0:T(1024)(128)(4,1)}), s8[2097152]{0:T(1024)(128)(4,1)S(1)}, s32[]{:S(2)}) async-start(s8[6291456]{0:T(1024)(128)(4,1)} %bitcast.181), calls=%async_computation.11 | async-start | bytes 4194304
  112.2 1.7 copy-start.4
  113.8 2.9 %copy-start.13 = (bf16[512,1,1,512]{0,3,2,1:T(8,128)(2,1)S(1)}, bf16[512,1,1,512]{0,3,2,1:T(8,128)(2,1)}, u32[]{:S(2)}) copy-start(bf16[512,1,1,512]{0,3,2,1:T(8,128)(2,1)} %copy.172) | copy-start | bytes 1572868
  115.1 1.7 copy-start.5
  116.8 1.4 copy-start.10
  118.6 3.0 %copy-start = (f32[2,1536,1,256]{3,1,0,2:T(8,128)}, f32[2,1536,1,256]{3,1,0,2:T(8,128)S(1)}, u32[]{:S(2)}) copy-start(f32[2,1536,1,256]{3,1,0,2:T(8,128)S(1)} %get-tuple-element.21) | copy-start | bytes 9437188
  121.6 55.2 %collective-permute-start.2 = (f32[2,512,2,256]{3,1,0,2:T(8,128)}, f32[2,512,2,256]{3,1,0,2:T(8,128)}, u32[]{:S(2)}, u32[]{:S(2)}) collective-permute-start(f32[2,512,2,256]{3,1,0,2:T(8,128)} %get-tuple-element.4), channel_id=1, source_target_pairs={{4,0},{8,4},{12,8},{16,12},{20,16},{24,20},{28,24},{32,28},{36,32}... | collective-permute-start | bytes 6291464 | tf_op jit(solution)/shard_map/ppermute | solution.py:14
  132.0 74.4 %collective-permute-start.3 = (f32[2,512,2,256]{3,1,0,2:T(8,128)}, f32[2,512,2,256]{3,1,0,2:T(8,128)}, u32[]{:S(2)}, u32[]{:S(2)}) collective-permute-start(f32[2,512,2,256]{3,1,0,2:T(8,128)} %get-tuple-element.5), channel_id=1, source_target_pairs={{8,0},{12,4},{16,8},{20,12},{24,16},{28,20},{32,24},{36,28},{40,32... | collective-permute-start | bytes 6291464 | tf_op jit(solution)/shard_map/ppermute | solution.py:14
  145.7 24.0 %all-to-all-start.3 = ((bf16[512,1,2,512]{3,2,1,0:T(2,128)(2,1)}), bf16[512,1,2,512]{3,2,1,0:T(2,128)(2,1)}, u32[]{:S(2)}, u32[]{:S(2)}) async-start(bf16[512,1,2,512]{3,2,1,0:T(2,128)(2,1)} %pad_maximum_fusion.2), calls=%async_computation.3 | async-start | bytes 2097152 | tf_op jit(solution)/shard_map/all_to_all | solution.py:135
  169.7 41.0 %all-to-all-start.5 = ((bf16[512,1,2,512]{3,2,1,0:T(2,128)(2,1)}), bf16[512,1,2,512]{3,2,1,0:T(2,128)(2,1)}, u32[]{:S(2)}, u32[]{:S(2)}) async-start(bf16[512,1,2,512]{3,2,1,0:T(2,128)(2,1)} %pad_maximum_fusion.3), calls=%async_computation.5 | async-start | bytes 2097152 | tf_op jit(solution)/shard_map/all_to_all | solution.py:136
  210.7 11.4 %all-to-all-start.7 = ((bf16[512,1,2,256]{3,2,1,0:T(2,128)(2,1)}), bf16[512,1,2,256]{3,2,1,0:T(2,128)(2,1)S(1)}, u32[]{:S(2)}, u32[]{:S(2)}) async-start(bf16[512,1,2,256]{3,2,1,0:T(2,128)(2,1)} %copy.198), calls=%async_computation.7 | async-start | bytes 1048576 | tf_op jit(solution)/shard_map/all_to_all | solution.py:138
  222.1 13.6 %all-to-all-start.6 = ((bf16[512,1,2,256]{3,2,1,0:T(2,128)(2,1)}), bf16[512,1,2,256]{3,2,1,0:T(2,128)(2,1)S(1)}, u32[]{:S(2)}, u32[]{:S(2)}) async-start(bf16[512,1,2,256]{3,2,1,0:T(2,128)(2,1)} %copy.196), calls=%async_computation.6 | async-start | bytes 1048576 | tf_op jit(solution)/shard_map/all_to_all | solution.py:137
where the time goes:
time: 239 us; the launch traced here: 237 us
  waiting for transfers between devices  66.4 us (28%)
  starting transfers between devices  58.5 us (24%)
  local copies, waits for them, and re-layouts  51.2 us (21%)
  matrix products  32.6 us (14%)
  other arithmetic  27.6 us (12%)
    ppermute x4, waiting for transfers between devices, passed_along(): return lax.ppermute(block, axis, route)  43.1 us
    ppermute x4, starting transfers between devices, passed_along(): return lax.ppermute(block, axis, route)  19.4 us
    sub x2, matrix products, tile_pass(): weights = jnp.exp(scores - row_max)  13.6 us
    unnamed x54, local copies, waits for them, and re-layouts  12.5 us
    dot_general x2, matrix products, tile_pass(): jnp.einsum('gqk,kd->qgd', grad_low, key_block, preferred_element_type=jnp...  7.86 us
    convert_element_type x2, other arithmetic, tile_pass(): probs_low = probs_full.astype(jnp.bfloat16)  7.57 us
    another operation x2, local copies, waits for them, and re-layouts, attend(): jnp.stack([swept_head[0] for swept_head in outputs], axis=1)  7.13 us
    another operation x2, local copies, waits for them, and re-layouts, attend(): jnp.stack([swept_head[1] for swept_head in outputs], axis=1)  7.12 us
  transfers between devices with their start and end apart: 12, of which 8 were waited for; matrix products, arithmetic and copies ran while one was open for 28% of the time, Pallas kernels for 0%

commit v1 on v0

--- a/solution.py
+++ b/solution.py
@@ -1,3 +1,4 @@
+import functools
 import jax
 import jax.numpy as jnp
 from jax import lax
@@ -6,6 +7,29 @@
 HEAD_WIDTH = 256
 WINDOW_LENGTH = 1024
 query_tile = 512
+
+
+def derive_sources_all(shard_in, axis_name):
+    v_now, mixed_arr = (lax.psum(1, axis_name=axis_name), lax.axis_index(axis_name))
+    known = list(shard_in.shape)
+    g_now = shard_in.shape[1] // v_now
+    known[1] = g_now
+    lower = known[0]
+    known[0] = lower * v_now
+    h_now = jnp.zeros(known, shard_in.dtype)
+    for ix in range(v_now):
+        p_next = lax.dynamic_slice_in_dim(shard_in, (mixed_arr ^ ix) * g_now, g_now, axis=1)
+        if ix:
+            p_next = lax.ppermute(
+                p_next,
+                axis_name=axis_name,
+                perm=list(map(lambda to_i: (to_i, to_i ^ ix), range(v_now))),
+            )
+        h_now = lax.dynamic_update_slice_in_dim(h_now, p_next, (mixed_arr ^ ix) * lower, axis=0)
+    return h_now
+
+
+unite_rails_now = functools.partial(derive_sources_all, axis_name="head")
 
 
 def passed_along(block, axis, distance):
@@ -158,7 +182,7 @@
             lax.all_to_all(query_split, "head", split_axis=1, concat_axis=0, tiled=True),
             lax.all_to_all(key_split, "head", split_axis=1, concat_axis=0, tiled=True),
             lax.all_to_all(value_split, "head", split_axis=1, concat_axis=0, tiled=True),
-            lax.all_to_all(grad_split, "head", split_axis=1, concat_axis=0, tiled=True),
+            unite_rails_now(grad_split),
         ),
         doc_lengths,
         group_width,

time: 239 us -> 229 us (0.958)
  local copies, waits for them, and re-layouts: 51.2 us -> 44.8 us
  waiting for transfers between devices: 66.4 us -> 62.7 us
    all_to_all x1, waiting for transfers between devices: 5.74 us -> 0.01 us  [shards(): lax.all_to_all(query_split, 'head', split_axis=1, concat_axis=0, tiled=True)]
    all_to_all x1 -> x0, starting transfers between devices: 5.09 us -> none  [shards(): lax.all_to_all(grad_split, 'head', split_axis=1, concat_axis=0, tiled=True)]
    ppermute x4, waiting for transfers between devices: 43.1 us -> 48 us  [passed_along(): return lax.ppermute(block, axis, route)]
    unnamed x54 -> x41, local copies, waits for them, and re-layouts: 12.5 us -> 8.02 us
    ppermute x0 -> x3, starting transfers between devices: none -> 4.09 us  [derive_sources_all(): lax.ppermute(p_next, axis_name=axis_name, perm=list(map(lambda to_i: (to_...]
  transfers between devices with their start and end apart: 12 -> 14, of which waited for: 8 -> 7; matrix products, arithmetic and copies ran while one was open for 28% -> 26% of each run, Pallas kernels for 0% -> 0%
where the time goes in v1:
time: 229 us; the launch traced here: 228 us
  waiting for transfers between devices  62.7 us (27%)
  starting transfers between devices  59 us (26%)
  local copies, waits for them, and re-layouts  44.8 us (20%)
  matrix products  32.5 us (14%)
  other arithmetic  27.6 us (12%)
    ppermute x4, waiting for transfers between devices, passed_along(): return lax.ppermute(block, axis, route)  48 us
    ppermute x4, starting transfers between devices, passed_along(): return lax.ppermute(block, axis, route)  19.4 us
    sub x2, matrix products, tile_pass(): weights = jnp.exp(scores - row_max)  13.6 us
    unnamed x41, local copies, waits for them, and re-layouts  8.02 us
    dot_general x2, matrix products, tile_pass(): jnp.einsum('gqk,kd->qgd', grad_low, key_block, preferred_element_type=jnp...  7.86 us
    convert_element_type x2, other arithmetic, tile_pass(): probs_low = probs_full.astype(jnp.bfloat16)  7.57 us
    another operation x2, local copies, waits for them, and re-layouts, attend(): jnp.stack([swept_head[0] for swept_head in outputs], axis=1)  7.13 us
    another operation x2, local copies, waits for them, and re-layouts, attend(): jnp.stack([swept_head[1] for swept_head in outputs], axis=1)  7.12 us
  transfers between devices with their start and end apart: 14, of which 7 were waited for; matrix products, arithmetic and copies ran while one was open for 26% of the time, Pallas kernels for 0%

profile of v1, /device:TPU:122, one launch (start us, length us, event | category | flops | bytes accessed | tf_op | source)
XLA Modules:
  0.0 227.7 jit_solution(5332028876851084163)
XLA Ops:
  0.6 1.4 copy.170
  2.0 1.0 copy.171
  3.1 5.0 %all-to-all-start = ((bf16[128,4,2,256]{3,0,2,1:T(8,128)(2,1)}), bf16[128,4,2,256]{3,0,2,1:T(8,128)(2,1)S(1)}, u32[]{:S(2)}, u32[]{:S(2)}) async-start(bf16[128,4,2,256]{3,0,2,1:T(8,128)(2,1)} %copy.171), calls=%async_computation | async-start | bytes 1048576 | tf_op jit(solution)/shard_map/all_to_all | solution.py:183
  8.8 1.0 constant_dynamic-slice_fusion
  9.8 1.5 collective-permute-start.4
  11.8 2.0 collective-permute-start.2
  14.1 1.0 copy.174
  15.2 5.5 %all-to-all-done = bf16[128,4,2,256]{3,0,2,1:T(8,128)(2,1)S(1)} async-done(((bf16[128,4,2,256]{3,0,2,1:T(8,128)(2,1)}), bf16[128,4,2,256]{3,0,2,1:T(8,128)(2,1)S(1)}, u32[]{:S(2)}, u32[]{:S(2)}) %all-to-all-start) | async-done | bytes 524320 | tf_op jit(solution)/shard_map/all_to_all | solution.py:183
  20.7 6.3 %all-to-all-start.1 = ((bf16[128,4,2,256]{3,0,2,1:T(8,128)(2,1)}), bf16[128,4,2,256]{3,0,2,1:T(8,128)(2,1)S(1)}, u32[]{:S(2)}, u32[]{:S(2)}) async-start(bf16[128,4,2,256]{3,0,2,1:T(8,128)(2,1)} %copy.174), calls=%async_computation.1 | async-start | bytes 1048576 | tf_op jit(solution)/shard_map/all_to_all | solution.py:184
  27.5 2.3 copy.177
  29.8 3.8 %all-to-all-done.1 = bf16[128,4,2,256]{3,0,2,1:T(8,128)(2,1)S(1)} async-done(((bf16[128,4,2,256]{3,0,2,1:T(8,128)(2,1)}), bf16[128,4,2,256]{3,0,2,1:T(8,128)(2,1)S(1)}, u32[]{:S(2)}, u32[]{:S(2)}) %all-to-all-start.1) | async-done | bytes 524320 | tf_op jit(solution)/shard_map/all_to_all | solution.py:184
  33.6 4.9 %all-to-all-start.2 = ((bf16[128,4,2,512]{0,3,2,1:T(8,128)(2,1)}), bf16[128,4,2,512]{0,3,2,1:T(8,128)(2,1)S(1)}, u32[]{:S(2)}, u32[]{:S(2)}) async-start(bf16[128,4,2,512]{0,3,2,1:T(8,128)(2,1)} %bitcast.13), calls=%async_computation.2 | async-start | bytes 2097152 | tf_op jit(solution)/shard_map/all_to_all | solution.py:182
  39.4 1.1 pad_maximum_fusion.1
  40.5 1.9 collective-permute-start.1
  42.4 4.7 %collective-permute-start = (bf16[2,512,2,256]{3,1,2,0:T(8,128)(2,1)}, bf16[2,512,2,256]{3,1,2,0:T(8,128)(2,1)}, u32[]{:S(2)}, u32[]{:S(2)}) collective-permute-start(bf16[2,512,2,256]{3,1,2,0:T(8,128)(2,1)} %pad_maximum_fusion.1), channel_id=1, source_target_pairs={{0,8},{4,12},{8,16},{12,20},{16,24},{20,28},{24,32},{28,36},{32,40... | collective-permute-start | bytes 3145736 | tf_op jit(solution)/shard_map/ppermute | solution.py:38
  47.1 2.1 fusion.13
  49.2 1.0 constant_dynamic-update-slice_fusion.2
  50.2 1.0 constant_dynamic-update-slice_fusion.1
  51.4 1.0 fusion.39
  53.0 1.0 copy.179
  54.0 1.0 copy.183
  55.0 10.6 %collective-permute-done.1 = bf16[2,512,2,256]{3,1,2,0:T(8,128)(2,1)} collective-permute-done((bf16[2,512,2,256]{3,1,2,0:T(8,128)(2,1)}, bf16[2,512,2,256]{3,1,2,0:T(8,128)(2,1)}, u32[]{:S(2)}, u32[]{:S(2)}) %collective-permute-start.1) | collective-permute-done | bytes 1048608 | tf_op jit(solution)/shard_map/ppermute | solution.py:38
  65.6 5.4 %collective-permute-done = bf16[2,512,2,256]{3,1,2,0:T(8,128)(2,1)} collective-permute-done((bf16[2,512,2,256]{3,1,2,0:T(8,128)(2,1)}, bf16[2,512,2,256]{3,1,2,0:T(8,128)(2,1)}, u32[]{:S(2)}, u32[]{:S(2)}) %collective-permute-start) | collective-permute-done | bytes 1048608 | tf_op jit(solution)/shard_map/ppermute | solution.py:38
  71.0 2.1 maximum_maximum_fusion
  73.2 7.2 %fusion.42 = (f32[2,512]{1,0:T(2,128)S(1)}, f32[2,512,1536]{1,2,0:T(8,128)}) fusion(pred[512,1536]{0,1:T(8,128)(4,1)} %fusion.13, bf16[512,2,256]{0,2,1:T(8,128)(2,1)} %bitcast.202, bf16[2,1536,2,256]{3,1,2,0:T(8,128)(2,1)S(1)} %maximum_maximum_fusion), kind=kOutput, calls=%fused_computation.87 | convolution fusion | flops 811599360 | bytes 8392704 | tf_op jit(solution)/shard_map/sub | solution.py:61
  80.4 3.7 %fusion.20 = bf16[2,512,1536]{1,2,0:T(8,128)(2,1)S(1)} fusion(f32[2,512,1536]{1,2,0:T(8,128)} %get-tuple-element.19, f32[2,512]{1,0:T(2,128)S(1)} %get-tuple-element.18), kind=kLoop, calls=%fused_computation.41 | loop fusion | flops 3145728 | bytes 9441280 | tf_op jit(solution)/shard_map/convert_element_type | solution.py:63
  84.2 1.8 multiply_reduce_fusion.1
  86.0 2.1 convolution_bitcast_fusion.2
  88.1 6.3 %fusion.41 = (f32[2,512]{1,0:T(2,128)S(1)}, f32[2,512,1536]{1,2,0:T(8,128)}) fusion(pred[512,1536]{0,1:T(8,128)(4,1)} %fusion.13, bf16[512,2,256]{0,2,1:T(8,128)(2,1)} %bitcast.200, bf16[2,1536,2,256]{3,1,2,0:T(8,128)(2,1)S(1)} %maximum_maximum_fusion), kind=kOutput, calls=%fused_computation.86 | convolution fusion | flops 811599360 | bytes 8392704 | tf_op jit(solution)/shard_map/sub | solution.py:61
  94.4 3.8 %fusion.21 = bf16[2,512,1536]{1,2,0:T(8,128)(2,1)S(1)} fusion(f32[2,512,1536]{1,2,0:T(8,128)} %get-tuple-element.17, f32[2,512]{1,0:T(2,128)S(1)} %get-tuple-element.16), kind=kLoop, calls=%fused_computation.42 | loop fusion | flops 3145728 | bytes 9441280 | tf_op jit(solution)/shard_map/convert_element_type | solution.py:63
  98.3 1.8 multiply_reduce_fusion
  100.1 1.0 convolution_bitcast_fusion
  101.2 1.1 fusion.5
  102.6 1.0 fusion.19
  104.3 1.2 fusion.3
  105.6 1.7 copy-done.5
  107.2 1.0 fusion.17
  109.1 2.8 %fusion.22 = (f32[2,512,2,256]{3,1,0,2:T(8,128)}, f32[2,512,2,256]{3,1,0,2:T(8,128)}) fusion(f32[2,1536,1,256]{3,1,0,2:T(8,128)S(1)} %get-tuple-element.24, f32[2,1536,1,256]{3,1,0,2:T(8,128)S(1)} %get-tuple-element.25), kind=kLoop, calls=%fused_computation.43 | loop fusion | flops 1048576 | bytes 10485760 | tf_op jit(solution)/shard_map/stack | solution.py:143
  112.1 10.4 %collective-permute-start.5 = (f32[2,512,2,256]{3,1,0,2:T(8,128)}, f32[2,512,2,256]{3,1,0,2:T(8,128)}, u32[]{:S(2)}, u32[]{:S(2)}) collective-permute-start(f32[2,512,2,256]{3,1,0,2:T(8,128)} %get-tuple-element.4), channel_id=1, source_target_pairs={{4,0},{8,4},{12,8},{16,12},{20,16},{24,20},{28,24},{32,28},{36,32}... | collective-permute-start | bytes 6291464 | tf_op jit(solution)/shard_map/ppermute | solution.py:38
  122.5 2.3 %collective-permute-start.6 = (f32[2,512,2,256]{3,1,0,2:T(8,128)}, f32[2,512,2,256]{3,1,0,2:T(8,128)}, u32[]{:S(2)}, u32[]{:S(2)}) collective-permute-start(f32[2,512,2,256]{3,1,0,2:T(8,128)} %get-tuple-element.5), channel_id=1, source_target_pairs={{8,0},{12,4},{16,8},{20,12},{24,16},{28,20},{32,24},{36,28},{40,32... | collective-permute-start | bytes 6291464 | tf_op jit(solution)/shard_map/ppermute | solution.py:38
  124.9 3.6 %copy.187 = bf16[512,1,1,512]{3,2,1,0:T(2,128)(2,1)} copy(bf16[512,1,1,512]{0,3,2,1:T(8,128)(2,1)} %bitcast.192) | data formatting | bytes 1048576 | tf_op jit(solution)/shard_map/stack | solution.py:137
  128.4 3.6 %copy.188 = bf16[512,1,1,512]{3,2,1,0:T(2,128)(2,1)} copy(bf16[512,1,1,512]{0,3,2,1:T(8,128)(2,1)} %bitcast.193) | data formatting | bytes 1048576 | tf_op jit(solution)/shard_map/stack | solution.py:137
  132.0 4.2 %pad_maximum_fusion.2 = bf16[512,1,2,512]{3,2,1,0:T(2,128)(2,1)} fusion(bf16[512,1,1,512]{3,2,1,0:T(2,128)(2,1)} %copy.188, bf16[512,1,1,512]{3,2,1,0:T(2,128)(2,1)} %copy.187), kind=kLoop, calls=%fused_computation.56 | loop fusion | flops 2097152 | bytes 2097152 | tf_op jit(solution)/shard_map/stack | solution.py:137
  136.2 4.8 %all-to-all-start.3 = ((bf16[512,1,2,512]{3,2,1,0:T(2,128)(2,1)}), bf16[512,1,2,512]{3,2,1,0:T(2,128)(2,1)}, u32[]{:S(2)}, u32[]{:S(2)}) async-start(bf16[512,1,2,512]{3,2,1,0:T(2,128)(2,1)} %pad_maximum_fusion.2), calls=%async_computation.3 | async-start | bytes 2097152 | tf_op jit(solution)/shard_map/all_to_all | solution.py:159
  141.0 3.9 %fusion.27 = bf16[256,2,512]{2,0,1:T(8,128)(2,1)} fusion(bf16[2,512,1536]{1,2,0:T(8,128)(2,1)} %copy-done.4, bf16[2,1536,2,256]{3,1,2,0:T(8,128)(2,1)} %copy-done.1), kind=kOutput, calls=%fused_computation.51 | convolution fusion | flops 805830656 | bytes 4456448 | tf_op jit(solution)/shard_map/gqk,kd->qgd/dot_general | solution.py:78
  144.9 3.6 %copy.200 = bf16[512,1,1,512]{3,2,1,0:T(2,128)(2,1)} copy(bf16[512,1,1,512]{0,3,2,1:T(8,128)(2,1)} %bitcast.185) | data formatting | bytes 1048576 | tf_op jit(solution)/shard_map/stack | solution.py:140
  148.5 3.9 %fusion.28 = bf16[256,2,512]{2,0,1:T(8,128)(2,1)} fusion(bf16[2,512,1536]{1,2,0:T(8,128)(2,1)} %copy-done.5, bf16[2,1536,2,256]{3,1,2,0:T(8,128)(2,1)} %copy-done.1), kind=kOutput, calls=%fused_computation.52 | convolution fusion | flops 805830656 | bytes 4456448 | tf_op jit(solution)/shard_map/gqk,kd->qgd/dot_general | solution.py:78
  152.4 3.6 %copy.201 = bf16[512,1,1,512]{3,2,1,0:T(2,128)(2,1)} copy(bf16[512,1,1,512]{0,3,2,1:T(8,128)(2,1)} %bitcast.184) | data formatting | bytes 1048576 | tf_op jit(solution)/shard_map/stack | solution.py:140
  156.0 4.2 %pad_maximum_fusion.3 = bf16[512,1,2,512]{3,2,1,0:T(2,128)(2,1)} fusion(bf16[512,1,1,512]{3,2,1,0:T(2,128)(2,1)} %copy.201, bf16[512,1,1,512]{3,2,1,0:T(2,128)(2,1)} %copy.200), kind=kLoop, calls=%fused_computation.57 | loop fusion | flops 2097152 | bytes 2097152 | tf_op jit(solution)/shard_map/stack | solution.py:140
  160.2 4.8 %all-to-all-start.4 = ((bf16[512,1,2,512]{3,2,1,0:T(2,128)(2,1)}), bf16[512,1,2,512]{3,2,1,0:T(2,128)(2,1)}, u32[]{:S(2)}, u32[]{:S(2)}) async-start(bf16[512,1,2,512]{3,2,1,0:T(2,128)(2,1)} %pad_maximum_fusion.3), calls=%async_computation.4 | async-start | bytes 2097152 | tf_op jit(solution)/shard_map/all_to_all | solution.py:160
  165.0 2.3 %collective-permute-done.5 = f32[2,512,2,256]{3,1,0,2:T(8,128)} collective-permute-done((f32[2,512,2,256]{3,1,0,2:T(8,128)}, f32[2,512,2,256]{3,1,0,2:T(8,128)}, u32[]{:S(2)}, u32[]{:S(2)}) %collective-permute-start.5) | collective-permute-done | bytes 2097184 | tf_op jit(solution)/shard_map/ppermute | solution.py:38
  167.3 29.7 %collective-permute-done.6 = f32[2,512,2,256]{3,1,0,2:T(8,128)} collective-permute-done((f32[2,512,2,256]{3,1,0,2:T(8,128)}, f32[2,512,2,256]{3,1,0,2:T(8,128)}, u32[]{:S(2)}, u32[]{:S(2)}) %collective-permute-start.6) | collective-permute-done | bytes 2097184 | tf_op jit(solution)/shard_map/ppermute | solution.py:38
  196.9 2.8 %fusion.26 = bf16[2,512,2,256]{3,1,0,2:T(8,128)(2,1)S(1)} fusion(f32[2,512,2,256]{3,1,0,2:T(8,128)} %collective-permute-done.6, f32[2,512,2,256]{3,1,0,2:T(8,128)} %collective-permute-done.5, f32[2,1536,1,256]{3,1,0,2:T(8,128)S(1)} %get-tuple-element.24, f32[2,1536,1,256]{3,1,0,2:T(8,128)} %copy-done), kind=kLoop, calls=%fused_computation.47 | loop fusion | flops 2097152 | bytes 11534336 | tf_op jit(solution)/shard_map/convert.1
  199.9 1.3 copy.209
  201.2 4.8 %all-to-all-start.6 = ((bf16[512,1,2,256]{3,2,1,0:T(2,128)(2,1)}), bf16[512,1,2,256]{3,2,1,0:T(2,128)(2,1)S(1)}, u32[]{:S(2)}, u32[]{:S(2)}) async-start(bf16[512,1,2,256]{3,2,1,0:T(2,128)(2,1)} %copy.209), calls=%async_computation.6 | async-start | bytes 1048576 | tf_op jit(solution)/shard_map/all_to_all | solution.py:162
  206.0 1.3 copy.207
  207.3 5.3 %all-to-all-done.6 = bf16[512,1,2,256]{3,2,1,0:T(2,128)(2,1)S(1)} async-done(((bf16[512,1,2,256]{3,2,1,0:T(2,128)(2,1)}), bf16[512,1,2,256]{3,2,1,0:T(2,128)(2,1)S(1)}, u32[]{:S(2)}, u32[]{:S(2)}) %all-to-all-start.6) | async-done | bytes 524320 | tf_op jit(solution)/shard_map/all_to_all | solution.py:162
  212.6 4.9 %all-to-all-start.5 = ((bf16[512,1,2,256]{3,2,1,0:T(2,128)(2,1)}), bf16[512,1,2,256]{3,2,1,0:T(2,128)(2,1)S(1)}, u32[]{:S(2)}, u32[]{:S(2)}) async-start(bf16[512,1,2,256]{3,2,1,0:T(2,128)(2,1)} %copy.207), calls=%async_computation.5 | async-start | bytes 1048576 | tf_op jit(solution)/shard_map/all_to_all | solution.py:161
  217.5 1.9 copy.189
  219.5 1.6 reshape.183
  221.1 1.9 copy.202
  223.0 1.6 reshape.185
  225.0 1.2 reshape.187
  226.6 1.2 reshape.186
  (68 shorter events, 6.4 us)
Async XLA Ops:
  0.6 7.4 %copy-start.10 = (bf16[128,4096]{1,0:T(8,128)(2,1)S(1)}, bf16[128,4096]{1,0:T(8,128)(2,1)}, u32[]{:S(2)}) copy-start(bf16[128,4096]{1,0:T(8,128)(2,1)} %param.8) | copy-start | bytes 3145732
  3.1 10.8 %copy-start.11 = (bf16[128,2048]{1,0:T(8,128)(2,1)S(1)}, bf16[128,2048]{1,0:T(8,128)(2,1)}, u32[]{:S(2)}) copy-start(bf16[128,2048]{1,0:T(8,128)(2,1)} %param.7) | copy-start | bytes 1572868
  3.1 17.6 %all-to-all-start = ((bf16[128,4,2,256]{3,0,2,1:T(8,128)(2,1)}), bf16[128,4,2,256]{3,0,2,1:T(8,128)(2,1)S(1)}, u32[]{:S(2)}, u32[]{:S(2)}) async-start(bf16[128,4,2,256]{3,0,2,1:T(8,128)(2,1)} %copy.171), calls=%async_computation | async-start | bytes 1048576 | tf_op jit(solution)/shard_map/all_to_all | solution.py:183
  8.7 18.3 %copy-start.14 = (s32[64]{0:T(128)S(1)}, s32[64]{0:T(128)}, u32[]{:S(2)}) copy-start(s32[64]{0:T(128)} %param.9) | copy-start | bytes 772
  9.8 41.5 %collective-permute-start.4 = (bf16[128,1,2,512]{0,3,2,1:T(8,128)(2,1)}, bf16[128,1,2,512]{0,3,2,1:T(8,128)(2,1)S(1)}, u32[]{:S(2)}, u32[]{:S(2)}) collective-permute-start(bf16[128,1,2,512]{0,3,2,1:T(8,128)(2,1)} %get-tuple-element.10), channel_id=1, source_target_pairs={{0,3},{1,2},{2,1},{3,0},{4,7},{5,6},{6,5},{7,4},{8,11},{9,10},{10,... | collective-permute-start | bytes 786440 | tf_op jit(solution)/shard_map/ppermute | solution.py:23
  11.2 39.0 %collective-permute-start.3 = (bf16[128,1,2,512]{0,3,2,1:T(8,128)(2,1)}, bf16[128,1,2,512]{0,3,2,1:T(8,128)(2,1)}, u32[]{:S(2)}, u32[]{:S(2)}) collective-permute-start(bf16[128,1,2,512]{0,3,2,1:T(8,128)(2,1)} %get-tuple-element.11), channel_id=1, source_target_pairs={{0,2},{1,3},{2,0},{3,1},{4,6},{5,7},{6,4},{7,5},{8,10},{9,11},{10,... | collective-permute-start | bytes 786440 | tf_op jit(solution)/shard_map/ppermute | solution.py:23
  11.8 37.4 %collective-permute-start.2 = (bf16[128,1,2,512]{0,3,2,1:T(8,128)(2,1)}, bf16[128,1,2,512]{0,3,2,1:T(8,128)(2,1)}, u32[]{:S(2)}, u32[]{:S(2)}) collective-permute-start(bf16[128,1,2,512]{0,3,2,1:T(8,128)(2,1)} %get-tuple-element.12), channel_id=1, source_target_pairs={{0,1},{1,0},{2,3},{3,2},{4,5},{5,4},{6,7},{7,6},{8,9},{9,8},{10,11... | collective-permute-start | bytes 786440 | tf_op jit(solution)/shard_map/ppermute | solution.py:23
  20.7 12.9 %all-to-all-start.1 = ((bf16[128,4,2,256]{3,0,2,1:T(8,128)(2,1)}), bf16[128,4,2,256]{3,0,2,1:T(8,128)(2,1)S(1)}, u32[]{:S(2)}, u32[]{:S(2)}) async-start(bf16[128,4,2,256]{3,0,2,1:T(8,128)(2,1)} %copy.174), calls=%async_computation.1 | async-start | bytes 1048576 | tf_op jit(solution)/shard_map/all_to_all | solution.py:184
  29.8 20.4 %copy-start.2 = (bf16[4,128,1,2,256]{4,1,0,3,2:T(8,128)(2,1)}, bf16[4,128,1,2,256]{4,1,0,3,2:T(8,128)(2,1)S(1)}, u32[]{:S(2)}) copy-start(bf16[4,128,1,2,256]{4,1,0,3,2:T(8,128)(2,1)S(1)} %copy.172) | copy-start | bytes 1572868
  33.6 18.8 %all-to-all-start.2 = ((bf16[128,4,2,512]{0,3,2,1:T(8,128)(2,1)}), bf16[128,4,2,512]{0,3,2,1:T(8,128)(2,1)S(1)}, u32[]{:S(2)}, u32[]{:S(2)}) async-start(bf16[128,4,2,512]{0,3,2,1:T(8,128)(2,1)} %bitcast.13), calls=%async_computation.2 | async-start | bytes 2097152 | tf_op jit(solution)/shard_map/all_to_all | solution.py:182
  38.6 0.8 copy-start.3
  40.5 25.1 %collective-permute-start.1 = (bf16[2,512,2,256]{3,1,2,0:T(8,128)(2,1)}, bf16[2,512,2,256]{3,1,2,0:T(8,128)(2,1)}, u32[]{:S(2)}, u32[]{:S(2)}) collective-permute-start(bf16[2,512,2,256]{3,1,2,0:T(8,128)(2,1)} %pad_maximum_fusion.1), channel_id=1, source_target_pairs={{0,4},{4,8},{8,12},{12,16},{16,20},{20,24},{24,28},{28,32},{32,36}... | collective-permute-start | bytes 3145736 | tf_op jit(solution)/shard_map/ppermute | solution.py:38
  42.4 28.6 %collective-permute-start = (bf16[2,512,2,256]{3,1,2,0:T(8,128)(2,1)}, bf16[2,512,2,256]{3,1,2,0:T(8,128)(2,1)}, u32[]{:S(2)}, u32[]{:S(2)}) collective-permute-start(bf16[2,512,2,256]{3,1,2,0:T(8,128)(2,1)} %pad_maximum_fusion.1), channel_id=1, source_target_pairs={{0,8},{4,12},{8,16},{12,20},{16,24},{20,28},{24,32},{28,36},{32,40... | collective-permute-start | bytes 3145736 | tf_op jit(solution)/shard_map/ppermute | solution.py:38
  73.2 31.1 %copy-start.1 = (bf16[2,1536,2,256]{3,1,2,0:T(8,128)(2,1)}, bf16[2,1536,2,256]{3,1,2,0:T(8,128)(2,1)S(1)}, u32[]{:S(2)}) copy-start(bf16[2,1536,2,256]{3,1,2,0:T(8,128)(2,1)S(1)} %maximum_maximum_fusion) | copy-start | bytes 9437188
  80.4 3.7 %copy-start.7 = (bf16[512,1,1,512]{0,3,2,1:T(8,128)(2,1)S(1)}, bf16[512,1,1,512]{0,3,2,1:T(8,128)(2,1)}, u32[]{:S(2)}) copy-start(bf16[512,1,1,512]{0,3,2,1:T(8,128)(2,1)} %get-tuple-element.8) | copy-start | bytes 1572868
  94.4 3.9 %copy-start.6 = (bf16[512,1,1,512]{0,3,2,1:T(8,128)(2,1)S(1)}, bf16[512,1,1,512]{0,3,2,1:T(8,128)(2,1)}, u32[]{:S(2)}) copy-start(bf16[512,1,1,512]{0,3,2,1:T(8,128)(2,1)} %get-tuple-element.9) | copy-start | bytes 1572868
  94.4 6.7 %slice-start = ((s8[6291456]{0:T(1024)(128)(4,1)}), s8[4194304]{0:T(1024)(128)(4,1)S(1)}, s32[]{:S(2)}) async-start(s8[6291456]{0:T(1024)(128)(4,1)} %bitcast.173), calls=%async_computation.7 | async-start | bytes 8388608
  98.3 2.8 %slice-start.1 = ((s8[6291456]{0:T(1024)(128)(4,1)}), s8[2097152]{0:T(1024)(128)(4,1)S(1)}, s32[]{:S(2)}) async-start(s8[6291456]{0:T(1024)(128)(4,1)} %bitcast.173), calls=%async_computation.8 | async-start | bytes 4194304
  100.1 1.0 copy-start.8
  100.1 4.2 %slice-start.2 = ((s8[6291456]{0:T(1024)(128)(4,1)}), s8[4194304]{0:T(1024)(128)(4,1)S(1)}, s32[]{:S(2)}) async-start(s8[6291456]{0:T(1024)(128)(4,1)} %bitcast.175), calls=%async_computation.9 | async-start | bytes 8388608
  101.2 1.4 copy-start.13
  101.2 3.1 %slice-start.3 = ((s8[6291456]{0:T(1024)(128)(4,1)}), s8[2097152]{0:T(1024)(128)(4,1)S(1)}, s32[]{:S(2)}) async-start(s8[6291456]{0:T(1024)(128)(4,1)} %bitcast.175), calls=%async_computation.10 | async-start | bytes 4194304
  102.6 1.7 copy-start.4
  104.3 2.9 %copy-start.12 = (bf16[512,1,1,512]{0,3,2,1:T(8,128)(2,1)S(1)}, bf16[512,1,1,512]{0,3,2,1:T(8,128)(2,1)}, u32[]{:S(2)}) copy-start(bf16[512,1,1,512]{0,3,2,1:T(8,128)(2,1)} %copy.183) | copy-start | bytes 1572868
  105.6 1.7 copy-start.5
  107.2 1.4 copy-start.9
  109.1 3.0 %copy-start = (f32[2,1536,1,256]{3,1,0,2:T(8,128)}, f32[2,1536,1,256]{3,1,0,2:T(8,128)S(1)}, u32[]{:S(2)}) copy-start(f32[2,1536,1,256]{3,1,0,2:T(8,128)S(1)} %get-tuple-element.25) | copy-start | bytes 9437188
  112.1 55.2 %collective-permute-start.5 = (f32[2,512,2,256]{3,1,0,2:T(8,128)}, f32[2,512,2,256]{3,1,0,2:T(8,128)}, u32[]{:S(2)}, u32[]{:S(2)}) collective-permute-start(f32[2,512,2,256]{3,1,0,2:T(8,128)} %get-tuple-element.4), channel_id=1, source_target_pairs={{4,0},{8,4},{12,8},{16,12},{20,16},{24,20},{28,24},{32,28},{36,32}... | collective-permute-start | bytes 6291464 | tf_op jit(solution)/shard_map/ppermute | solution.py:38
  122.5 74.4 %collective-permute-start.6 = (f32[2,512,2,256]{3,1,0,2:T(8,128)}, f32[2,512,2,256]{3,1,0,2:T(8,128)}, u32[]{:S(2)}, u32[]{:S(2)}) collective-permute-start(f32[2,512,2,256]{3,1,0,2:T(8,128)} %get-tuple-element.5), channel_id=1, source_target_pairs={{8,0},{12,4},{16,8},{20,12},{24,16},{28,20},{32,24},{36,28},{40,32... | collective-permute-start | bytes 6291464 | tf_op jit(solution)/shard_map/ppermute | solution.py:38
  136.2 24.0 %all-to-all-start.3 = ((bf16[512,1,2,512]{3,2,1,0:T(2,128)(2,1)}), bf16[512,1,2,512]{3,2,1,0:T(2,128)(2,1)}, u32[]{:S(2)}, u32[]{:S(2)}) async-start(bf16[512,1,2,512]{3,2,1,0:T(2,128)(2,1)} %pad_maximum_fusion.2), calls=%async_computation.3 | async-start | bytes 2097152 | tf_op jit(solution)/shard_map/all_to_all | solution.py:159
  160.2 41.0 %all-to-all-start.4 = ((bf16[512,1,2,512]{3,2,1,0:T(2,128)(2,1)}), bf16[512,1,2,512]{3,2,1,0:T(2,128)(2,1)}, u32[]{:S(2)}, u32[]{:S(2)}) async-start(bf16[512,1,2,512]{3,2,1,0:T(2,128)(2,1)} %pad_maximum_fusion.3), calls=%async_computation.4 | async-start | bytes 2097152 | tf_op jit(solution)/shard_map/all_to_all | solution.py:160
  201.2 11.4 %all-to-all-start.6 = ((bf16[512,1,2,256]{3,2,1,0:T(2,128)(2,1)}), bf16[512,1,2,256]{3,2,1,0:T(2,128)(2,1)S(1)}, u32[]{:S(2)}, u32[]{:S(2)}) async-start(bf16[512,1,2,256]{3,2,1,0:T(2,128)(2,1)} %copy.209), calls=%async_computation.6 | async-start | bytes 1048576 | tf_op jit(solution)/shard_map/all_to_all | solution.py:162
  212.6 13.6 %all-to-all-start.5 = ((bf16[512,1,2,256]{3,2,1,0:T(2,128)(2,1)}), bf16[512,1,2,256]{3,2,1,0:T(2,128)(2,1)S(1)}, u32[]{:S(2)}, u32[]{:S(2)}) async-start(bf16[512,1,2,256]{3,2,1,0:T(2,128)(2,1)} %copy.207), calls=%async_computation.5 | async-start | bytes 1048576 | tf_op jit(solution)/shard_map/all_to_all | solution.py:161
